TPU v7x, 512 devices: a whole 4x4x16 slice. The times are simulated.
512 devices in a mesh: blk: 64 (over y, z_lo, core), group: 8 (over x, z_hi).
Axes of the slice: x: 4, y: 4, z: 16 (z_hi: 2, z_lo: 8; z = z_hi * 8 + z_lo), core: 2. Of those that a mesh axis runs over, the one named last changes fastest.
Arguments:
- audio_embed: float32 [49152, 512], P('blk'), may hold values from -4 to 4
- text_embed: float32 [49152, 512], P(('blk', 'group')), may hold values from -4 to 4
Outputs:
- grad_audio: float32 [49152, 512], P(('blk', 'group'))
- grad_text: float32 [49152, 512], P(('blk', 'group'))
- loss_rows: float32 [49152], P(('blk', 'group'))
- loss_cols: float32 [49152], P(('blk', 'group'))
All inputs are finite; a program needn't handle non-finite values.
Results may differ from a plain program's by a relative error of at most 0.0003.
Values sent between devices are 32-bit elements; how exact they have to be, the bound alone decides.
No kernel may reach another device: no remote copies, remote signals or barrier semaphores. Data moves between devices by JAX's collectives and lax.ppermute only.
A program may use at most 64 MiB of HBM per device.

v0:
```python
import jax
import jax.numpy as jnp
from jax import lax
from jax.sharding import PartitionSpec as P

SPAN = 3
logit_scale = 1.0 / 0.07
precise = lax.Precision.HIGHEST


def shifted(value, axis, by):
    devices = lax.axis_size(axis)
    return lax.ppermute(value, axis, [(i, (i + by) % devices) for i in range(devices)])


def send_ahead(payload):
    return shifted(payload, "blk", -1)


def send_back(payload):
    return shifted(payload, "blk", 1)


def pair_merge(earlier, later):
    highest = jnp.maximum(earlier[0], later[0])
    return (
        highest,
        earlier[1] * jnp.exp(earlier[0] - highest) + later[1] * jnp.exp(later[0] - highest),
    )


def shards(audio_embed, text_embed):
    row_count = audio_embed.shape[0]
    text_rows = text_embed.shape[0]
    member = lax.axis_index("group")
    text_tiles = [text_embed]
    moving = text_embed
    for _ in range(SPAN - 1):
        moving = send_ahead(moving)
        text_tiles.append(moving)
    window = jnp.stack(text_tiles)
    logits = logit_scale * jnp.einsum("rd,kcd->rkc", audio_embed, window, precision=precise)
    local_max = jnp.max(logits, axis=(1, 2))
    row_max = lax.pmax(local_max, "group")
    row_total = lax.psum(jnp.sum(jnp.exp(logits - row_max[:, None, None]), axis=(1, 2)), "group")
    row_lse = row_max + jnp.log(row_total)
    col_max = jnp.max(logits, axis=0)
    col_sum = jnp.sum(jnp.exp(logits - col_max[None]), axis=0)
    carried = (col_max[SPAN - 1], col_sum[SPAN - 1])
    for offset in range(SPAN - 2, -1, -1):
        arrived = send_back(carried)
        carried = pair_merge(arrived, (col_max[offset], col_sum[offset]))
    col_lse = carried[0] + jnp.log(carried[1])
    lse_tiles = [col_lse]
    moving = col_lse
    for _ in range(SPAN - 1):
        moving = send_ahead(moving)
        lse_tiles.append(moving)
    lse_window = jnp.stack(lse_tiles)
    soft_weights = 0.5 * (
        jnp.exp(logits - row_lse[:, None, None]) + jnp.exp(logits - lse_window[None])
    )
    row_ids = lax.broadcasted_iota(jnp.int32, (row_count, SPAN, text_rows), 0)
    tile_ids = lax.broadcasted_iota(jnp.int32, (row_count, SPAN, text_rows), 1)
    col_ids = lax.broadcasted_iota(jnp.int32, (row_count, SPAN, text_rows), 2)
    positive = ((tile_ids == 0) & (row_ids == member * text_rows + col_ids)).astype(jnp.float32)
    grad_logits = soft_weights - positive
    text_parts = logit_scale * jnp.einsum(
        "rkc,rd->kcd", grad_logits, audio_embed, precision=precise
    )
    grad_sum = text_parts[SPAN - 1]
    for offset in range(SPAN - 2, -1, -1):
        grad_sum = send_back(grad_sum) + text_parts[offset]
    own_logits = lax.dynamic_slice_in_dim(logits[:, 0, :], member * text_rows, text_rows, 0)
    positive_scores = jnp.diagonal(own_logits)
    own_lse = lax.dynamic_slice_in_dim(row_lse, member * text_rows, text_rows, 0)
    loss_rows = own_lse - positive_scores
    loss_cols = col_lse - positive_scores
    grad_audio = lax.psum_scatter(
        logit_scale * jnp.einsum("rkc,kcd->rd", grad_logits, window, precision=precise),
        "group",
        scatter_dimension=0,
        tiled=True,
    )
    return (grad_audio, grad_sum, loss_rows, loss_cols)


def solution(mesh):
    placed = (P("blk", None), P(("blk", "group"), None))
    return jax.shard_map(
        shards,
        mesh=mesh,
        in_specs=placed,
        out_specs=(
            P(("blk", "group"), None),
            P(("blk", "group"), None),
            P(("blk", "group")),
            P(("blk", "group")),
        ),
        check_vma=False,
    )
```

profile of v0, /device:TPU:8, one launch (start us, length us, event | category | flops | bytes accessed | tf_op | source)
XLA Modules:
  0.0 297.5 jit_solution(14635427026608289326)
XLA Ops:
  7.2 0.0 reduce-scatter.2.cloned.1.call-start
  7.2 12.6 %collective-permute-start = (f32[96,512]{1,0:T(8,128)}, f32[96,512]{1,0:T(8,128)S(1)}, u32[]{:S(2)}, u32[]{:S(2)}) collective-permute-start(f32[96,512]{1,0:T(8,128)} %param.3), channel_id=1, source_target_pairs={{0,504},{8,0},{16,8},{24,16},{32,24},{40,32},{48,40},{56,48},{64,5... | collective-permute-start | bytes 589832 | tf_op jit(solution)/shard_map/ppermute | solution.py:13
  19.8 3.5 %collective-permute-done = f32[96,512]{1,0:T(8,128)S(1)} collective-permute-done((f32[96,512]{1,0:T(8,128)}, f32[96,512]{1,0:T(8,128)S(1)}, u32[]{:S(2)}, u32[]{:S(2)}) %collective-permute-start) | collective-permute-done | bytes 196640 | tf_op jit(solution)/shard_map/ppermute | solution.py:13
  23.3 11.2 %collective-permute-start.1 = (f32[96,512]{1,0:T(8,128)S(1)}, f32[96,512]{1,0:T(8,128)S(1)}, u32[]{:S(2)}, u32[]{:S(2)}) collective-permute-start(f32[96,512]{1,0:T(8,128)S(1)} %collective-permute-done), channel_id=1, source_target_pairs={{0,504},{8,0},{16,8},{24,16},{32,24},{40,32},{48,40},{56,48},{64,5... | collective-permute-start | bytes 589832 | tf_op jit(solution)/shard_map/ppermute | solution.py:13
  34.6 3.2 %collective-permute-done.1 = f32[96,512]{1,0:T(8,128)S(1)} collective-permute-done((f32[96,512]{1,0:T(8,128)S(1)}, f32[96,512]{1,0:T(8,128)S(1)}, u32[]{:S(2)}, u32[]{:S(2)}) %collective-permute-start.1) | collective-permute-done | bytes 196640 | tf_op jit(solution)/shard_map/ppermute | solution.py:13
  37.8 2.6 fusion.26
  40.4 42.0 %pmax.7 = f32[768]{0:T(1024)S(1)} all-reduce(f32[768]{0:T(1024)S(1)} %get-tuple-element.11), channel_id=1, replica_groups=mesh['blk'=64,'group'=8] {'group'}, use_global_device_ids=true, to_apply=%region_1.0 | all-reduce | flops 768 | bytes 6144 | tf_op jit(solution)/shard_map/pmax | solution.py:44
  82.4 0.2 exponential_reduce_fusion.1
  82.6 0.3 exponential_reduce_fusion
  83.0 1.9 collective-permute-start.2
  84.9 1.9 collective-permute-start.4
  86.8 35.9 %psum.7 = f32[768]{0:T(1024)S(1)} all-reduce(f32[768]{0:T(1024)S(1)} %get-tuple-element.4), channel_id=1, replica_groups=mesh['blk'=64,'group'=8] {'group'}, use_global_device_ids=true, to_apply=%region_3.0 | all-reduce | flops 768 | bytes 6144 | tf_op jit(solution)/shard_map/psum | solution.py:45
  122.8 1.9 collective-permute-start.5
  124.7 1.9 collective-permute-start.3
  126.6 0.1 dynamic-slice_bitcast_fusion
  126.7 1.3 gather_fusion
  128.0 7.2 %collective-permute-done.5 = f32[96]{0:T(128)S(1)} collective-permute-done((f32[96]{0:T(128)S(1)}, f32[96]{0:T(128)S(1)}, u32[]{:S(2)}, u32[]{:S(2)}) %collective-permute-start.5) | collective-permute-done | bytes 416 | tf_op jit(solution)/shard_map/ppermute | solution.py:13
  135.2 1.9 collective-permute-done.3
  137.1 0.6 fusion.24
  137.7 2.1 collective-permute-start.6
  139.8 1.3 collective-permute-done.6
  141.0 11.1 %collective-permute-start.7 = (f32[96]{0:T(128)S(1)}, f32[96]{0:T(128)S(1)}, u32[]{:S(2)}, u32[]{:S(2)}) collective-permute-start(f32[96]{0:T(128)S(1)} %collective-permute-done.6), channel_id=1, source_target_pairs={{0,504},{8,0},{16,8},{24,16},{32,24},{40,32},{48,40},{56,48},{64,5... | collective-permute-start | bytes 1160 | tf_op jit(solution)/shard_map/ppermute | solution.py:13
  152.2 1.3 collective-permute-done.7
  153.4 4.2 %bitcast_multiply_fusion = f32[768,512]{1,0:T(8,128)} fusion(f32[1,96,512]{2,1,0:T(8,128)S(1)} %bitcast.90, f32[1,96,512]{2,1,0:T(8,128)S(1)} %bitcast.88, f32[1,96,512]{2,1,0:T(8,128)S(1)} %bitcast.86, s32[96]{0:T(128)S(1)} %iota_add_fusion, f32[3,96]{1,0:T(4,128)S(1)} %pad_maximum_fusion.3, f32[768]{0:T(1024)S(1)} %log_add_fusion, ...), kind=kOutput, calls=%fused_computation.1 | convolution fusion | flops 1361412096 | bytes 3052035 | tf_op jit(solution)/shard_map/rkc,kcd->rd/dot_general | solution.py:80
  157.6 0.0 reduce-scatter.2.cloned.1.call-update
  157.6 2.0 fusion.7
  159.7 1.9 collective-permute-start.8
  161.6 12.6 %collective-permute-done.8 = f32[96,512]{1,0:T(8,128)S(1)} collective-permute-done((f32[96,512]{1,0:T(8,128)S(1)}, f32[96,512]{1,0:T(8,128)S(1)}, u32[]{:S(2)}, u32[]{:S(2)}) %collective-permute-start.8) | collective-permute-done | bytes 196640 | tf_op jit(solution)/shard_map/ppermute | solution.py:13
  174.2 1.9 collective-permute-start.9
  176.1 20.8 %collective-permute-done.9 = f32[96,512]{1,0:T(8,128)S(1)} collective-permute-done((f32[96,512]{1,0:T(8,128)S(1)}, f32[96,512]{1,0:T(8,128)S(1)}, u32[]{:S(2)}, u32[]{:S(2)}) %collective-permute-start.9) | collective-permute-done | bytes 196640 | tf_op jit(solution)/shard_map/ppermute | solution.py:13
  196.9 0.7 fusion.11
  197.7 93.0 %reduce-scatter.2.cloned.1.call-done = f32[96,512]{1,0:T(8,128)} async-done(((f32[768,512]{1,0:T(8,128)}), f32[96,512]{1,0:T(8,128)}) %reduce-scatter.2.cloned.1.call-update) | async-done | bytes 196624 | tf_op jit(solution)/shard_map/reduce_scatter | solution.py:79
  (17 shorter events, 0.1 us)
Async XLA Ops:
  7.2 30.6 %copy-start = (f32[768,512]{1,0:T(8,128)S(1)}, f32[768,512]{1,0:T(8,128)}, u32[]{:S(2)}) copy-start(f32[768,512]{1,0:T(8,128)} %param.2) | copy-start | bytes 4718596
  7.2 283.5 %reduce-scatter.2.cloned.1.call-start = ((), (), s32[]{:S(2)}) async-start(), calls=%async_computation.1 | async-start | bytes 1769472 | tf_op jit(solution)/shard_map/reduce_scatter | solution.py:79
  7.2 16.1 %collective-permute-start = (f32[96,512]{1,0:T(8,128)}, f32[96,512]{1,0:T(8,128)S(1)}, u32[]{:S(2)}, u32[]{:S(2)}) collective-permute-start(f32[96,512]{1,0:T(8,128)} %param.3), channel_id=1, source_target_pairs={{0,504},{8,0},{16,8},{24,16},{32,24},{40,32},{48,40},{56,48},{64,5... | collective-permute-start | bytes 589832 | tf_op jit(solution)/shard_map/ppermute | solution.py:13
  23.3 14.4 %collective-permute-start.1 = (f32[96,512]{1,0:T(8,128)S(1)}, f32[96,512]{1,0:T(8,128)S(1)}, u32[]{:S(2)}, u32[]{:S(2)}) collective-permute-start(f32[96,512]{1,0:T(8,128)S(1)} %collective-permute-done), channel_id=1, source_target_pairs={{0,504},{8,0},{16,8},{24,16},{32,24},{40,32},{48,40},{56,48},{64,5... | collective-permute-start | bytes 589832 | tf_op jit(solution)/shard_map/ppermute | solution.py:13
  40.4 113.1 %copy-start.1 = (f32[96,512]{1,0:T(8,128)S(1)}, f32[96,512]{1,0:T(8,128)}, u32[]{:S(2)}) copy-start(f32[96,512]{1,0:T(8,128)} %param.3) | copy-start | bytes 589828
  83.0 39.8 %collective-permute-start.2 = (f32[96]{0:T(128)S(1)}, f32[96]{0:T(128)S(1)}, u32[]{:S(2)}, u32[]{:S(2)}) collective-permute-start(f32[96]{0:T(128)S(1)} %slice_bitcast_fusion.4), channel_id=1, source_target_pairs={{0,8},{8,16},{16,24},{24,32},{32,40},{40,48},{48,56},{56,64},{64,7... | collective-permute-start | bytes 1160 | tf_op jit(solution)/shard_map/ppermute | solution.py:13
  84.9 37.8 %collective-permute-start.4 = (f32[96]{0:T(128)S(1)}, f32[96]{0:T(128)S(1)}, u32[]{:S(2)}, u32[]{:S(2)}) collective-permute-start(f32[96]{0:T(128)S(1)} %slice_bitcast_fusion.3), channel_id=1, source_target_pairs={{0,8},{8,16},{16,24},{24,32},{32,40},{40,48},{48,56},{56,64},{64,7... | collective-permute-start | bytes 1160 | tf_op jit(solution)/shard_map/ppermute | solution.py:13
  122.8 12.4 %collective-permute-start.5 = (f32[96]{0:T(128)S(1)}, f32[96]{0:T(128)S(1)}, u32[]{:S(2)}, u32[]{:S(2)}) collective-permute-start(f32[96]{0:T(128)S(1)} %get-tuple-element.9), channel_id=1, source_target_pairs={{0,8},{8,16},{16,24},{24,32},{32,40},{40,48},{48,56},{56,64},{64,7... | collective-permute-start | bytes 1160 | tf_op jit(solution)/shard_map/ppermute | solution.py:13
  124.7 12.4 %collective-permute-start.3 = (f32[96]{0:T(128)S(1)}, f32[96]{0:T(128)S(1)}, u32[]{:S(2)}, u32[]{:S(2)}) collective-permute-start(f32[96]{0:T(128)S(1)} %get-tuple-element.8), channel_id=1, source_target_pairs={{0,8},{8,16},{16,24},{24,32},{32,40},{40,48},{48,56},{56,64},{64,7... | collective-permute-start | bytes 1160 | tf_op jit(solution)/shard_map/ppermute | solution.py:13
  137.7 3.4 %collective-permute-start.6 = (f32[96]{0:T(128)S(1)}, f32[96]{0:T(128)S(1)}, u32[]{:S(2)}, u32[]{:S(2)}) collective-permute-start(f32[96]{0:T(128)S(1)} %get-tuple-element.7), channel_id=1, source_target_pairs={{0,504},{8,0},{16,8},{24,16},{32,24},{40,32},{48,40},{56,48},{64,5... | collective-permute-start | bytes 1160 | tf_op jit(solution)/shard_map/ppermute | solution.py:13
  141.0 12.4 %collective-permute-start.7 = (f32[96]{0:T(128)S(1)}, f32[96]{0:T(128)S(1)}, u32[]{:S(2)}, u32[]{:S(2)}) collective-permute-start(f32[96]{0:T(128)S(1)} %collective-permute-done.6), channel_id=1, source_target_pairs={{0,504},{8,0},{16,8},{24,16},{32,24},{40,32},{48,40},{56,48},{64,5... | collective-permute-start | bytes 1160 | tf_op jit(solution)/shard_map/ppermute | solution.py:13
  159.7 14.5 %collective-permute-start.8 = (f32[96,512]{1,0:T(8,128)S(1)}, f32[96,512]{1,0:T(8,128)S(1)}, u32[]{:S(2)}, u32[]{:S(2)}) collective-permute-start(f32[96,512]{1,0:T(8,128)S(1)} %slice_bitcast_fusion.2), channel_id=1, source_target_pairs={{0,8},{8,16},{16,24},{24,32},{32,40},{40,48},{48,56},{56,64},{64,7... | collective-permute-start | bytes 589832 | tf_op jit(solution)/shard_map/ppermute | solution.py:13
  174.2 22.8 %collective-permute-start.9 = (f32[96,512]{1,0:T(8,128)S(1)}, f32[96,512]{1,0:T(8,128)S(1)}, u32[]{:S(2)}, u32[]{:S(2)}) collective-permute-start(f32[96,512]{1,0:T(8,128)S(1)} %fusion.12), channel_id=1, source_target_pairs={{0,8},{8,16},{16,24},{24,32},{32,40},{40,48},{48,56},{56,64},{64,7... | collective-permute-start | bytes 589832 | tf_op jit(solution)/shard_map/ppermute | solution.py:13
Sparse Core Ops, SparseCore 0:
  157.8 132.8 reduce-scatter.1
where the time goes:
time: 298 us; the launch traced here: 297 us
  waiting for transfers between devices  145 us (49%)
  blocking collectives  77.9 us (26%)
  starting transfers between devices  48.6 us (16%)
  between operations  14.2 us (5%)
  matrix products  8.73 us (3%)
    reduce_scatter x1, waiting for transfers between devices, shards(): lax.psum_scatter(logit_scale * jnp.einsum('rkc,kcd->rd', grad_logits, win...  93 us
    ppermute x10, waiting for transfers between devices, shifted(): lax.ppermute(value, axis, [(i, (i + by) % devices) for i in range(devices)])  51.7 us
    ppermute x10, starting transfers between devices, shifted(): lax.ppermute(value, axis, [(i, (i + by) % devices) for i in range(devices)])  48.5 us
    pmax x1, blocking collectives, shards(): row_max = lax.pmax(local_max, 'group')  42 us
    psum x1, blocking collectives, shards(): lax.psum(jnp.sum(jnp.exp(logits - row_max[:, None, None]), axis=(1, 2)),...  35.9 us
  transfers between devices with their start and end apart: 11, of which 9 were waited for; matrix products, arithmetic and copies ran while one was open for 1% of the time, Pallas kernels for 0%

commit v1 on v0

--- a/solution.py
+++ b/solution.py
@@ -42,7 +42,9 @@
     logits = logit_scale * jnp.einsum("rd,kcd->rkc", audio_embed, window, precision=precise)
     local_max = jnp.max(logits, axis=(1, 2))
     row_max = lax.pmax(local_max, "group")
-    row_total = lax.psum(jnp.sum(jnp.exp(logits - row_max[:, None, None]), axis=(1, 2)), "group")
+    part = jnp.sum(jnp.exp(logits - row_max[:, None, None]), axis=(1, 2))
+    pieces = lax.all_gather(part, "group", axis=0, tiled=False)
+    row_total = pieces.sum(axis=0)
     row_lse = row_max + jnp.log(row_total)
     col_max = jnp.max(logits, axis=0)
     col_sum = jnp.sum(jnp.exp(logits - col_max[None]), axis=0)

time: 298 us -> 325 us (1.091)
  blocking collectives: 77.9 us -> 105 us
    all_gather x0 -> x1, blocking collectives: none -> 63.1 us  [shards(): pieces = lax.all_gather(part, 'group', axis=0, tiled=False)]
    psum x1 -> x0, blocking collectives: 35.9 us -> none  [shards(): lax.psum(jnp.sum(jnp.exp(logits - row_max[:, None, None]), axis=(1, 2)),...]
where the time goes in v1:
time: 325 us
  waiting for transfers between devices  145 us (45%)
  blocking collectives  105 us (32%)
  starting transfers between devices  48.6 us (15%)
  between operations  14.2 us (4%)
  matrix products  8.73 us (3%)
    reduce_scatter x1, waiting for transfers between devices, shards(): lax.psum_scatter(logit_scale * jnp.einsum('rkc,kcd->rd', grad_logits, win...  93.3 us
    all_gather x1, blocking collectives, shards(): pieces = lax.all_gather(part, 'group', axis=0, tiled=False)  63.1 us
    ppermute x10, waiting for transfers between devices, shifted(): lax.ppermute(value, axis, [(i, (i + by) % devices) for i in range(devices)])  51.5 us
    ppermute x10, starting transfers between devices, shifted(): lax.ppermute(value, axis, [(i, (i + by) % devices) for i in range(devices)])  48.5 us
    pmax x1, blocking collectives, shards(): row_max = lax.pmax(local_max, 'group')  41.9 us
  transfers between devices with their start and end apart: 11, of which 9 were waited for; matrix products, arithmetic and copies ran while one was open for 1% of the time, Pallas kernels for 0%

profile of v1, /device:TPU:8, one launch (start us, length us, event | category | flops | bytes accessed | tf_op | source)
XLA Modules:
  0.0 324.6 jit_solution(7437538481984118051)
XLA Ops:
  7.2 0.0 reduce-scatter.2.cloned.1.call-start
  7.2 12.6 %collective-permute-start = (f32[96,512]{1,0:T(8,128)}, f32[96,512]{1,0:T(8,128)S(1)}, u32[]{:S(2)}, u32[]{:S(2)}) collective-permute-start(f32[96,512]{1,0:T(8,128)} %param.3), channel_id=1, source_target_pairs={{0,504},{8,0},{16,8},{24,16},{32,24},{40,32},{48,40},{56,48},{64,5... | collective-permute-start | bytes 589832 | tf_op jit(solution)/shard_map/ppermute | solution.py:13
  19.8 3.5 %collective-permute-done = f32[96,512]{1,0:T(8,128)S(1)} collective-permute-done((f32[96,512]{1,0:T(8,128)}, f32[96,512]{1,0:T(8,128)S(1)}, u32[]{:S(2)}, u32[]{:S(2)}) %collective-permute-start) | collective-permute-done | bytes 196640 | tf_op jit(solution)/shard_map/ppermute | solution.py:13
  23.3 11.2 %collective-permute-start.1 = (f32[96,512]{1,0:T(8,128)S(1)}, f32[96,512]{1,0:T(8,128)S(1)}, u32[]{:S(2)}, u32[]{:S(2)}) collective-permute-start(f32[96,512]{1,0:T(8,128)S(1)} %collective-permute-done), channel_id=1, source_target_pairs={{0,504},{8,0},{16,8},{24,16},{32,24},{40,32},{48,40},{56,48},{64,5... | collective-permute-start | bytes 589832 | tf_op jit(solution)/shard_map/ppermute | solution.py:13
  34.6 3.3 %collective-permute-done.1 = f32[96,512]{1,0:T(8,128)S(1)} collective-permute-done((f32[96,512]{1,0:T(8,128)S(1)}, f32[96,512]{1,0:T(8,128)S(1)}, u32[]{:S(2)}, u32[]{:S(2)}) %collective-permute-start.1) | collective-permute-done | bytes 196640 | tf_op jit(solution)/shard_map/ppermute | solution.py:13
  37.8 2.6 fusion.26
  40.4 41.9 %pmax.7 = f32[768]{0:T(1024)S(1)} all-reduce(f32[768]{0:T(1024)S(1)} %get-tuple-element.11), channel_id=1, replica_groups=mesh['blk'=64,'group'=8] {'group'}, use_global_device_ids=true, to_apply=%region_1.0 | all-reduce | flops 768 | bytes 6144 | tf_op jit(solution)/shard_map/pmax | solution.py:44
  82.3 0.2 exponential_reduce_fusion.1
  82.5 0.3 exponential_reduce_fusion
  82.8 1.9 collective-permute-start.2
  84.8 1.9 collective-permute-start.4
  86.7 63.1 %all-gather.1 = f32[8,1,768]{2,1,0:T(1,128)S(1)} all-gather(f32[1,1,768]{2,1,0:T(1,128)S(1)} %reshape.20), channel_id=2, replica_groups=mesh['blk'=64,'group'=8] {'group'}, dimensions={0}, use_global_device_ids=true | all-gather | bytes 27648 | tf_op jit(solution)/shard_map/all_gather | solution.py:46
  149.9 1.9 collective-permute-start.5
  151.8 1.9 collective-permute-start.3
  153.8 0.1 dynamic-slice_bitcast_fusion
  153.8 1.3 gather_fusion
  155.1 7.2 %collective-permute-done.5 = f32[96]{0:T(128)S(1)} collective-permute-done((f32[96]{0:T(128)S(1)}, f32[96]{0:T(128)S(1)}, u32[]{:S(2)}, u32[]{:S(2)}) %collective-permute-start.5) | collective-permute-done | bytes 416 | tf_op jit(solution)/shard_map/ppermute | solution.py:13
  162.3 1.9 collective-permute-done.3
  164.2 0.6 fusion.24
  164.8 2.1 collective-permute-start.6
  166.9 1.3 collective-permute-done.6
  168.2 11.1 %collective-permute-start.7 = (f32[96]{0:T(128)S(1)}, f32[96]{0:T(128)S(1)}, u32[]{:S(2)}, u32[]{:S(2)}) collective-permute-start(f32[96]{0:T(128)S(1)} %collective-permute-done.6), channel_id=1, source_target_pairs={{0,504},{8,0},{16,8},{24,16},{32,24},{40,32},{48,40},{56,48},{64,5... | collective-permute-start | bytes 1160 | tf_op jit(solution)/shard_map/ppermute | solution.py:13
  179.3 1.3 collective-permute-done.7
  180.6 4.2 %bitcast_multiply_fusion = f32[768,512]{1,0:T(8,128)} fusion(f32[1,96,512]{2,1,0:T(8,128)S(1)} %bitcast.90, f32[1,96,512]{2,1,0:T(8,128)S(1)} %bitcast.88, f32[1,96,512]{2,1,0:T(8,128)S(1)} %bitcast.86, s32[96]{0:T(128)S(1)} %iota_add_fusion, f32[3,96]{1,0:T(4,128)S(1)} %pad_maximum_fusion.3, f32[768]{0:T(1024)S(1)} %log_add_fusion, ...), kind=kOutput, calls=%fused_computation.1 | convolution fusion | flops 1361412096 | bytes 3052035 | tf_op jit(solution)/shard_map/rkc,kcd->rd/dot_general | solution.py:82
  184.7 0.0 reduce-scatter.2.cloned.1.call-update
  184.8 2.0 fusion.7
  186.8 1.9 collective-permute-start.8
  188.7 12.6 %collective-permute-done.8 = f32[96,512]{1,0:T(8,128)S(1)} collective-permute-done((f32[96,512]{1,0:T(8,128)S(1)}, f32[96,512]{1,0:T(8,128)S(1)}, u32[]{:S(2)}, u32[]{:S(2)}) %collective-permute-start.8) | collective-permute-done | bytes 196640 | tf_op jit(solution)/shard_map/ppermute | solution.py:13
  201.3 1.9 collective-permute-start.9
  203.2 20.6 %collective-permute-done.9 = f32[96,512]{1,0:T(8,128)S(1)} collective-permute-done((f32[96,512]{1,0:T(8,128)S(1)}, f32[96,512]{1,0:T(8,128)S(1)}, u32[]{:S(2)}, u32[]{:S(2)}) %collective-permute-start.9) | collective-permute-done | bytes 196640 | tf_op jit(solution)/shard_map/ppermute | solution.py:13
  223.8 0.7 fusion.11
  224.5 93.3 %reduce-scatter.2.cloned.1.call-done = f32[96,512]{1,0:T(8,128)} async-done(((f32[768,512]{1,0:T(8,128)}), f32[96,512]{1,0:T(8,128)}) %reduce-scatter.2.cloned.1.call-update) | async-done | bytes 196624 | tf_op jit(solution)/shard_map/reduce_scatter | solution.py:81
  (19 shorter events, 0.2 us)
Async XLA Ops:
  7.2 30.7 %copy-start = (f32[768,512]{1,0:T(8,128)S(1)}, f32[768,512]{1,0:T(8,128)}, u32[]{:S(2)}) copy-start(f32[768,512]{1,0:T(8,128)} %param.2) | copy-start | bytes 4718596
  7.2 310.6 %reduce-scatter.2.cloned.1.call-start = ((), (), s32[]{:S(2)}) async-start(), calls=%async_computation.1 | async-start | bytes 1769472 | tf_op jit(solution)/shard_map/reduce_scatter | solution.py:81
  7.2 16.1 %collective-permute-start = (f32[96,512]{1,0:T(8,128)}, f32[96,512]{1,0:T(8,128)S(1)}, u32[]{:S(2)}, u32[]{:S(2)}) collective-permute-start(f32[96,512]{1,0:T(8,128)} %param.3), channel_id=1, source_target_pairs={{0,504},{8,0},{16,8},{24,16},{32,24},{40,32},{48,40},{56,48},{64,5... | collective-permute-start | bytes 589832 | tf_op jit(solution)/shard_map/ppermute | solution.py:13
  23.3 14.5 %collective-permute-start.1 = (f32[96,512]{1,0:T(8,128)S(1)}, f32[96,512]{1,0:T(8,128)S(1)}, u32[]{:S(2)}, u32[]{:S(2)}) collective-permute-start(f32[96,512]{1,0:T(8,128)S(1)} %collective-permute-done), channel_id=1, source_target_pairs={{0,504},{8,0},{16,8},{24,16},{32,24},{40,32},{48,40},{56,48},{64,5... | collective-permute-start | bytes 589832 | tf_op jit(solution)/shard_map/ppermute | solution.py:13
  82.3 98.3 %copy-start.1 = (f32[96,512]{1,0:T(8,128)S(1)}, f32[96,512]{1,0:T(8,128)}, u32[]{:S(2)}) copy-start(f32[96,512]{1,0:T(8,128)} %param.3) | copy-start | bytes 589828
  82.8 67.0 %collective-permute-start.2 = (f32[96]{0:T(128)S(1)}, f32[96]{0:T(128)S(1)}, u32[]{:S(2)}, u32[]{:S(2)}) collective-permute-start(f32[96]{0:T(128)S(1)} %slice_bitcast_fusion.4), channel_id=1, source_target_pairs={{0,8},{8,16},{16,24},{24,32},{32,40},{40,48},{48,56},{56,64},{64,7... | collective-permute-start | bytes 1160 | tf_op jit(solution)/shard_map/ppermute | solution.py:13
  84.8 65.1 %collective-permute-start.4 = (f32[96]{0:T(128)S(1)}, f32[96]{0:T(128)S(1)}, u32[]{:S(2)}, u32[]{:S(2)}) collective-permute-start(f32[96]{0:T(128)S(1)} %slice_bitcast_fusion.3), channel_id=1, source_target_pairs={{0,8},{8,16},{16,24},{24,32},{32,40},{40,48},{48,56},{56,64},{64,7... | collective-permute-start | bytes 1160 | tf_op jit(solution)/shard_map/ppermute | solution.py:13
  149.9 12.4 %collective-permute-start.5 = (f32[96]{0:T(128)S(1)}, f32[96]{0:T(128)S(1)}, u32[]{:S(2)}, u32[]{:S(2)}) collective-permute-start(f32[96]{0:T(128)S(1)} %get-tuple-element.9), channel_id=1, source_target_pairs={{0,8},{8,16},{16,24},{24,32},{32,40},{40,48},{48,56},{56,64},{64,7... | collective-permute-start | bytes 1160 | tf_op jit(solution)/shard_map/ppermute | solution.py:13
  151.8 12.4 %collective-permute-start.3 = (f32[96]{0:T(128)S(1)}, f32[96]{0:T(128)S(1)}, u32[]{:S(2)}, u32[]{:S(2)}) collective-permute-start(f32[96]{0:T(128)S(1)} %get-tuple-element.8), channel_id=1, source_target_pairs={{0,8},{8,16},{16,24},{24,32},{32,40},{40,48},{48,56},{56,64},{64,7... | collective-permute-start | bytes 1160 | tf_op jit(solution)/shard_map/ppermute | solution.py:13
  164.8 3.4 %collective-permute-start.6 = (f32[96]{0:T(128)S(1)}, f32[96]{0:T(128)S(1)}, u32[]{:S(2)}, u32[]{:S(2)}) collective-permute-start(f32[96]{0:T(128)S(1)} %get-tuple-element.7), channel_id=1, source_target_pairs={{0,504},{8,0},{16,8},{24,16},{32,24},{40,32},{48,40},{56,48},{64,5... | collective-permute-start | bytes 1160 | tf_op jit(solution)/shard_map/ppermute | solution.py:13
  168.2 12.4 %collective-permute-start.7 = (f32[96]{0:T(128)S(1)}, f32[96]{0:T(128)S(1)}, u32[]{:S(2)}, u32[]{:S(2)}) collective-permute-start(f32[96]{0:T(128)S(1)} %collective-permute-done.6), channel_id=1, source_target_pairs={{0,504},{8,0},{16,8},{24,16},{32,24},{40,32},{48,40},{56,48},{64,5... | collective-permute-start | bytes 1160 | tf_op jit(solution)/shard_map/ppermute | solution.py:13
  186.8 14.5 %collective-permute-start.8 = (f32[96,512]{1,0:T(8,128)S(1)}, f32[96,512]{1,0:T(8,128)S(1)}, u32[]{:S(2)}, u32[]{:S(2)}) collective-permute-start(f32[96,512]{1,0:T(8,128)S(1)} %slice_bitcast_fusion.2), channel_id=1, source_target_pairs={{0,8},{8,16},{16,24},{24,32},{32,40},{40,48},{48,56},{56,64},{64,7... | collective-permute-start | bytes 589832 | tf_op jit(solution)/shard_map/ppermute | solution.py:13
  201.3 22.5 %collective-permute-start.9 = (f32[96,512]{1,0:T(8,128)S(1)}, f32[96,512]{1,0:T(8,128)S(1)}, u32[]{:S(2)}, u32[]{:S(2)}) collective-permute-start(f32[96,512]{1,0:T(8,128)S(1)} %fusion.12), channel_id=1, source_target_pairs={{0,8},{8,16},{16,24},{24,32},{32,40},{40,48},{48,56},{56,64},{64,7... | collective-permute-start | bytes 589832 | tf_op jit(solution)/shard_map/ppermute | solution.py:13
Sparse Core Ops, SparseCore 0:
  184.9 132.8 reduce-scatter.1
